TPU v7x, 512 devices: a whole 4x8x8 slice. The times are simulated.
512 devices in a mesh: dp: 128 (over y, z, core), feat: 4 (over x).
Axes of the slice: x: 4, y: 8, z: 8, core: 2. Of those that a mesh axis runs over, the one named last changes fastest.
Arguments:
- activations: bfloat16 [131072, 8192], P('dp', 'feat'), may hold values from -6 to 6
- cand_index: int32 [131072], P('dp'), may hold values from 0 to 127
- labels: int32 [8192], P('dp'), may hold values 0 or 1
- counts: int32 [128], P('dp'), may hold values from 1 to 64, as said below
Outputs:
- scores: float32 [131072, 128], P('dp', 'feat')
Inputs may be any that keep to these rules, and one draw needn't show every extreme that they name: `counts`: the fullest slab has all 64 prompt slots live.
All inputs are finite; a program needn't handle non-finite values. No bound on the sum of `labels` on one device may be relied on, other than what follows from the above.
Results may differ from a plain program's by a relative error of at most 0.0047.
Values may be sent and summed in bfloat16 or wider, within the bound.
A program may use at most 64 MiB of HBM per device.

v0:
```python
import jax
import jax.numpy as jnp
from jax import lax
from jax.sharding import PartitionSpec as P

CAND_DEV = 1
PER_PROMPT = 16


epsilon = 1e-06


def project(activations, dir_block):
    return lax.dot_general(
        activations, dir_block, (((1,), (1,)), ((), ())), preferred_element_type=jnp.float32
    )


def per_device(activations, cand_index, labels, counts):
    row_total = activations.shape[0]
    cand_total = CAND_DEV * lax.axis_size("dp")
    prompt_of = jnp.arange(row_total, dtype=jnp.int32) // PER_PROMPT
    live = prompt_of < counts[0]
    classes = jnp.repeat(labels, PER_PROMPT)
    cand_ids = jnp.arange(cand_total, dtype=jnp.int32)
    matches = (cand_index[None, :] == cand_ids[:, None]) & live[None, :]
    harmful_hits = matches & (classes[None, :] == 1)
    harmless_hits = matches & (classes[None, :] == 0)
    member = jnp.concatenate([harmful_hits, harmless_hits], axis=0).astype(jnp.bfloat16)
    class_sums = jnp.dot(member, activations, preferred_element_type=jnp.float32).reshape(
        2, cand_total, -1
    )
    class_counts = jnp.sum(member.astype(jnp.float32), axis=1).reshape(2, cand_total)
    owned_sums, owned_counts = (
        lax.psum_scatter(class_sums, "dp", scatter_dimension=1, tiled=True),
        lax.psum_scatter(class_counts, "dp", scatter_dimension=1, tiled=True),
    )
    harmful_mean = owned_sums[0] / jnp.maximum(owned_counts[0], 1.0)[:, None]
    harmless_mean = owned_sums[1] / jnp.maximum(owned_counts[1], 1.0)[:, None]
    raw_float = harmful_mean - harmless_mean
    raw_dir = raw_float.astype(jnp.bfloat16)
    squares = jnp.sum(jnp.square(raw_dir.astype(jnp.float32)), axis=1)
    total_sq = lax.psum(squares, "feat")
    inv_norm = lax.rsqrt(total_sq + epsilon).astype(jnp.bfloat16)
    dir_block = lax.all_gather(raw_dir, "dp", axis=0, tiled=True)
    inv_block = lax.all_gather(inv_norm, "dp", axis=0, tiled=True)
    partial_value = project(activations, dir_block) * inv_block.astype(jnp.float32)[None, :]
    return lax.psum_scatter(partial_value, "feat", scatter_dimension=1, tiled=True)


def solution(mesh):
    return jax.shard_map(
        per_device,
        mesh=mesh,
        in_specs=(P("dp", "feat"), P("dp"), P("dp"), P("dp")),
        out_specs=P("dp", "feat"),
        check_vma=False,
    )
```

profile of v0, /device:TPU:1, one launch (start us, length us, event | category | flops | bytes accessed | tf_op | source)
XLA Modules:
  0.0 618.5 jit_solution(13851311557933916579)
XLA Ops:
  6.5 0.0 all-reduce.5.cloned.1.call-start
  6.5 0.7 broadcast_compare_fusion.1
  7.2 0.1 broadcast_in_dim.4
  7.3 0.1 eq.43
  7.4 0.1 broadcast_in_dim.5
  7.4 0.1 eq.45
  8.2 0.9 fusion.5
  9.1 3.4 fusion.6
  12.5 0.0 copy-start
  12.5 2.9 copy.8
  15.4 0.0 all-reduce.5.cloned.1.call-update
  15.5 0.0 reduce-scatter.3.cloned.1.call-start
  15.5 0.0 copy-done
  15.5 0.6 fusion.12
  16.1 0.2 convert_reduce_fusion
  16.3 254.9 %all-reduce.2 = f32[2,128]{1,0:T(2,128)S(1)} all-reduce(f32[2,128]{1,0:T(2,128)S(1)} %bitcast.23), channel_id=4, replica_groups=mesh['dp'=128,'feat'=4] {'dp'}, use_global_device_ids=true, to_apply=%region_2.3.clone | all-reduce | flops 256 | bytes 2048
  271.2 0.7 constant_dynamic-slice_fusion
  271.9 0.6 fusion.13
  273.8 0.0 all-reduce.5.cloned.1.call-done
  273.8 2.0 multiply_reduce_fusion
  275.8 9.0 %psum.7 = f32[1]{0:T(128)} all-reduce(f32[1]{0:T(128)} %bitcast.6), channel_id=1, replica_groups=mesh['dp'=128,'feat'=4] {'feat'}, use_global_device_ids=true, to_apply=%region_4.5 | all-reduce | flops 1 | bytes 8 | tf_op jit(solution)/shard_map/psum | solution.py:43
  286.1 1.3 dynamic-update-slice
  287.4 253.7 %all-reduce = bf16[128]{0:T(256)(128)(2,1)S(1)} all-reduce(bf16[128]{0:T(256)(128)(2,1)S(1)} %dynamic-update-slice), channel_id=1, replica_groups=mesh['dp'=128,'feat'=4] {'dp'}, use_global_device_ids=true, to_apply=%add | all-reduce | flops 128 | bytes 512
  541.1 47.8 %all-gather = bf16[128,1,2048]{2,1,0:T(2,128)(2,1)S(1)} all-gather(bf16[1,1,2048]{2,1,0:T(2,128)(2,1)S(1)} %bitcast.22), channel_id=2, replica_groups=mesh['dp'=128,'feat'=4] {'dp'}, dimensions={0}, use_global_device_ids=true | all-gather | bytes 528384 | tf_op jit(solution)/shard_map/all_gather | solution.py:45
  589.0 4.6 fusion
  593.5 0.0 reduce-scatter.3.cloned.1.call-update
  593.6 18.1 %reduce-scatter.3.cloned.1.call-done = f32[1024,32]{0,1:T(8,128)} async-done(((f32[1024,128]{0,1:T(8,128)}), f32[1024,32]{0,1:T(8,128)}) %reduce-scatter.3.cloned.1.call-update) | async-done | bytes 131088 | tf_op jit(solution)/shard_map/reduce_scatter | solution.py:48
  (3 shorter events, 0.0 us)
Async XLA Ops:
  6.5 267.3 %all-reduce.5.cloned.1.call-start = ((), (), s32[]{:S(2)}) async-start(), calls=%async_computation.2 | async-start | bytes 4194304
  12.5 3.0 copy-start
  15.5 596.2 %reduce-scatter.3.cloned.1.call-start = ((), (), s32[]{:S(2)}) async-start(), calls=%async_computation.1 | async-start | bytes 655360 | tf_op jit(solution)/shard_map/reduce_scatter | solution.py:48
Sparse Core Ops, SparseCore 0:
  15.6 206.1 all-reduce.4
  593.7 17.9 reduce-scatter.2
where the time goes:
time: 620 us; the launch traced here: 618 us
  blocking collectives  566 us (91%)
  waiting for transfers between devices  18.1 us (3%)
  between operations  16.6 us (3%)
  matrix products  8.01 us (1%)
  local copies, waits for them, and re-layouts  6.46 us (1%)
    unnamed x2, blocking collectives  509 us
    all_gather x1, blocking collectives, per_device(): dir_block = lax.all_gather(raw_dir, 'dp', axis=0, tiled=True)  47.8 us
    reduce_scatter x1, waiting for transfers between devices, per_device(): lax.psum_scatter(partial_value, 'feat', scatter_dimension=1, tiled=True)  18.1 us
  transfers between devices with their start and end apart: 2, of which 1 were waited for; matrix products, arithmetic and copies ran while one was open for 0% of the time, Pallas kernels for 0%

commit v1 on v0

v1 whole, which is shorter than its diff:
```python
import functools

import jax
import jax.numpy as jnp
from jax import lax
from jax.experimental import pallas as pl
from jax.experimental.pallas import tpu as pltpu
from jax.sharding import PartitionSpec as P

CANDS = 128
PER_PROMPT = 16
EPSILON = 1e-06
MESH = pl.DeviceIdType.MESH
NT = (((1,), (1,)), ((), ()))


def order_of(n):
    return sorted(range(1, n), key=lambda k: -min(k, n - k))


def kernel(
    n, nx, act_ref, cand_ref, label_ref, live_ref, out_ref,
    act, member, xsend, xrecv, mine, part, ring, part2, ring2, unit, dirs, flat,
    proj, prec, cnt, cntr, sq, sqr,
    act_sem, cs, cr, xs, xr, s1, r1, s2, r2, g2s, g2r, g1s, g1r, gcs, gcr,
    ps, pr, qs, qr,
):
    rows, width = act_ref.shape
    half = width // 2
    cols = half // 2
    cu, fu = CANDS // n, half // n
    xb = CANDS // nx

    dp = lax.axis_index("dp")
    x = lax.axis_index("feat")
    c = lax.rem(dp, 2)
    z = lax.rem(dp // 2, n)
    y = dp // (2 * n)

    def at(yy, zz, cc, xx):
        return ((yy * n + zz) * 2 + cc, xx)

    other = 1 - c

    def along(axis, k):
        if axis == "y":
            return at(lax.rem(y + k, n), z, c, x)
        if axis == "z":
            return at(y, lax.rem(z + k, n), c, x)
        if axis == "x":
            return at(y, z, c, lax.rem(x + k, nx))
        if axis == "a":
            return at(
                lax.rem(y + other * k, n), lax.rem(z + c * k, n), c, x
            )
        return at(lax.rem(y + c * k, n), lax.rem(z + other * k, n), c, x)

    a = other * y + c * z
    b = other * z + c * y
    peer = at(y, z, other, x)

    def remote(src, dst, ss, rs, to):
        return pltpu.make_async_remote_copy(
            src_ref=src, dst_ref=dst, send_sem=ss, recv_sem=rs,
            device_id=to, device_id_type=MESH,
        )

    barrier = pltpu.get_barrier_semaphore()
    pl.semaphore_signal(barrier, inc=1, device_id=peer, device_id_type=MESH)
    for axis, size in (("y", n), ("z", n), ("x", nx)):
        for k in range(1, size):
            pl.semaphore_signal(
                barrier, inc=1, device_id=along(axis, k), device_id_type=MESH
            )

    loads = []
    for t in range(4):
        q = lax.rem(other * 2 + t, 4)
        load = pltpu.make_async_copy(
            act_ref.at[:, pl.ds(pl.multiple_of(q * cols, cols), cols)],
            act.at[q], act_sem.at[t],
        )
        load.start()
        loads.append((q, load))

    prompts = label_ref.shape[1]
    lab = label_ref[...]
    slot = lax.broadcasted_iota(jnp.int32, (8, prompts), 1)
    kind = lax.broadcasted_iota(jnp.int32, (8, prompts), 0)
    wanted = (lab == 1 - kind) & (kind < 2) & (slot < live_ref[...])
    by_prompt = jnp.where(wanted, 1.0, 0.0).astype(jnp.bfloat16)
    spread = jnp.where(
        lax.broadcasted_iota(jnp.int32, (prompts, rows), 1) // PER_PROMPT
        == lax.broadcasted_iota(jnp.int32, (prompts, rows), 0), 1.0, 0.0,
    ).astype(jnp.bfloat16)
    by_row = jnp.dot(by_prompt, spread, preferred_element_type=jnp.float32)
    hit = jnp.where(
        cand_ref[...] == lax.broadcasted_iota(jnp.int32, (CANDS, rows), 0), 1.0, 0.0
    )
    cnt[0] = lax.dot_general(
        by_row.astype(jnp.bfloat16), hit.astype(jnp.bfloat16), NT,
        preferred_element_type=jnp.float32,
    )
    member[0:CANDS, :] = (hit * by_row[0:1, :]).astype(jnp.bfloat16)
    member[CANDS:, :] = (hit * by_row[1:2, :]).astype(jnp.bfloat16)

    pl.semaphore_wait(barrier, 1 + 2 * (n - 1) + nx - 1)

    pending = []
    copy = remote(cnt.at[0], cntr.at[0], cs.at[0], cr.at[0], peer)
    copy.start()
    pending.append(copy)

    pair = []
    for t in range(2):
        q, load = loads[t]
        load.wait()
        xsend[t] = jnp.dot(
            member[...], act[q], preferred_element_type=jnp.float32
        )
        copy = remote(xsend.at[t], xrecv.at[t], xs.at[t], xr.at[t], peer)
        copy.start()
        pair.append(copy)
        if t == 0:
            pending[0].wait_recv()
            cnt[1] = cnt[0] + cntr[0]
            for k in order_of(n):
                copy = remote(
                    cnt.at[1], cntr.at[k], cs.at[k], cr.at[k], along("y", k)
                )
                copy.start()
                pending.append(copy)

    for t in range(2):
        q, load = loads[2 + t]
        load.wait()
        mine[t] = jnp.dot(
            member[...], act[q], preferred_element_type=jnp.float32
        )
        if t == 0:
            total = cnt[1]
            for copy in pending[1:]:
                copy.wait_recv()
            for k in range(1, n):
                total = total + cntr[k]
            cnt[2] = total
            for k in order_of(n):
                copy = remote(
                    cnt.at[2], cntr.at[n - 1 + k], cs.at[n - 1 + k],
                    cr.at[n - 1 + k], along("z", k),
                )
                copy.start()
                pending.append(copy)

    for copy in pending[n:]:
        copy.wait_recv()
    total = cnt[2]
    for k in range(n, 2 * n - 1):
        total = total + cntr[k]
    scale = 1.0 / jnp.maximum(total, 1.0)
    eye = (
        lax.broadcasted_iota(jnp.int32, (CANDS, CANDS), 0)
        == lax.broadcasted_iota(jnp.int32, (CANDS, CANDS), 1)
    )
    harmful = jnp.sum(jnp.where(eye, scale[0:1, :], 0.0), axis=1, keepdims=True)
    harmless = jnp.sum(jnp.where(eye, scale[1:2, :], 0.0), axis=1, keepdims=True)

    for t in range(2):
        pair[t].wait_recv()
        diff = (
            (mine[t, 0:CANDS, :] + xrecv[t, 0:CANDS, :]) * harmful
            - (mine[t, CANDS:, :] + xrecv[t, CANDS:, :]) * harmless
        )
        for i in range(n):
            for jj in range(n // 2):
                j = t * (n // 2) + jj
                u = other * (i * n + j) + c * (j * n + i)
                part[u] = diff[i * cu:(i + 1) * cu, jj * fu:(jj + 1) * fu]

    first = []
    for k in order_of(n):
        to = lax.rem(a + k, n)
        copy = remote(
            part.at[pl.ds(to * n, n)], ring.at[k], s1.at[k], r1.at[k], along("a", k)
        )
        copy.start()
        first.append(copy)
    for copy in first:
        copy.wait_recv()
    for u in range(n):
        total = part[a * n + u]
        for k in range(1, n):
            total = total + ring[k, u]
        part2[u] = total

    second = []
    for k in order_of(n):
        to = lax.rem(b + k, n)
        copy = remote(part2.at[to], ring2.at[k], s2.at[k], r2.at[k], along("b", k))
        copy.start()
        second.append(copy)
    for copy in second:
        copy.wait_recv()
    total = part2[b]
    for k in range(1, n):
        total = total + ring2[k]
    dirs[c, a * n + b] = total.astype(jnp.bfloat16)

    third = []
    for k in order_of(n):
        here = dirs.at[c, a * n + b]
        copy = remote(here, here, g2s.at[k], g2r.at[k], along("b", k))
        copy.start()
        third.append(copy)
    for copy in third:
        copy.wait_recv()
    fourth = []
    here = dirs.at[c, pl.ds(a * n, n)]
    for k in order_of(n):
        copy = remote(here, here, g1s.at[k], g1r.at[k], along("a", k))
        copy.start()
        fourth.append(copy)
    for copy in fourth:
        copy.wait_recv()
    across = remote(dirs.at[c], dirs.at[c], gcs.at[0], gcr.at[0], peer)
    across.start()
    across.wait_recv()

    squares = jnp.zeros((CANDS, 1), jnp.float32)
    for h in range(2):
        for i in range(n):
            for j in range(n):
                u = i * n + j if h == 0 else j * n + i
                flat[i * cu:(i + 1) * cu, h * half + j * fu:h * half + (j + 1) * fu] = (
                    dirs[h, u]
                )
    full = flat[...].astype(jnp.float32)
    squares = jnp.sum(full * full, axis=1, keepdims=True)
    sq[...] = jnp.broadcast_to(
        jnp.sum(jnp.where(eye, squares, 0.0), axis=0, keepdims=True), (8, CANDS)
    )
    squared = []
    for k in order_of(nx):
        copy = remote(sq, sqr.at[k], qs.at[k], qr.at[k], along("x", k))
        copy.start()
        squared.append(copy)

    parts = proj.shape[0]
    span = rows // parts
    sent = []
    for t in range(parts):
        total = jnp.zeros((CANDS, span), jnp.float32)
        for q in range(4):
            total = total + lax.dot_general(
                flat[:, q * cols:(q + 1) * cols],
                act[q, t * span:(t + 1) * span, :], NT,
                preferred_element_type=jnp.float32,
            )
        for k in range(nx):
            proj[t, k] = total[k * xb:(k + 1) * xb, :]
        for k in order_of(nx):
            to = lax.rem(x + k, nx)
            copy = remote(
                proj.at[t, to], prec.at[t, k], ps.at[t, k], pr.at[t, k],
                along("x", k),
            )
            copy.start()
            sent.append(copy)

    for copy in squared:
        copy.wait_recv()
    total = sq[...]
    for k in range(1, nx):
        total = total + sqr[k]
    inv = lax.rsqrt(total[0:1, :] + EPSILON).astype(jnp.bfloat16).astype(jnp.float32)
    own = (
        lax.broadcasted_iota(jnp.int32, (xb, CANDS), 0) + x * xb
        == lax.broadcasted_iota(jnp.int32, (xb, CANDS), 1)
    )
    inv = jnp.sum(jnp.where(own, inv, 0.0), axis=1, keepdims=True)
    for t in range(parts):
        for copy in sent[t * (nx - 1):(t + 1) * (nx - 1)]:
            copy.wait_recv()
        total = proj[t, x]
        for k in range(1, nx):
            total = total + prec[t, k]
        out_ref[:, t * span:(t + 1) * span] = total * inv

    for copy in [
        *pending, *pair, *first, *second, *third, *fourth, across, *squared, *sent
    ]:
        copy.wait_send()


def per_device(n, nx, activations, cand_index, labels, counts):
    rows, width = activations.shape
    half = width // 2
    cols = half // 2
    cu, fu = CANDS // n, half // n
    xb = CANDS // nx
    parts = 2
    f32, bf16, dma = jnp.float32, jnp.bfloat16, pltpu.SemaphoreType.DMA
    vmem = pl.BlockSpec(memory_space=pltpu.VMEM)
    out = pl.pallas_call(
        functools.partial(kernel, n, nx),
        out_shape=jax.ShapeDtypeStruct((xb, rows), f32),
        in_specs=[pl.BlockSpec(memory_space=pltpu.HBM), vmem, vmem, vmem],
        out_specs=vmem,
        scratch_shapes=[
            pltpu.VMEM((4, rows, cols), bf16),
            pltpu.VMEM((2 * CANDS, rows), bf16),
            pltpu.VMEM((2, 2 * CANDS, cols), f32),
            pltpu.VMEM((2, 2 * CANDS, cols), f32),
            pltpu.VMEM((2, 2 * CANDS, cols), f32),
            pltpu.VMEM((n * n, cu, fu), f32),
            pltpu.VMEM((n, n, cu, fu), f32),
            pltpu.VMEM((n, cu, fu), f32),
            pltpu.VMEM((n, cu, fu), f32),
            pltpu.VMEM((cu, fu), f32),
            pltpu.VMEM((2, n * n, cu, fu), bf16),
            pltpu.VMEM((CANDS, width), bf16),
            pltpu.VMEM((parts, nx, xb, rows // parts), f32),
            pltpu.VMEM((parts, nx, xb, rows // parts), f32),
            pltpu.VMEM((3, 8, CANDS), f32),
            pltpu.VMEM((2 * n - 1, 8, CANDS), f32),
            pltpu.VMEM((8, CANDS), f32),
            pltpu.VMEM((nx, 8, CANDS), f32),
            dma((4,)), dma((2 * n - 1,)), dma((2 * n - 1,)), dma((2,)), dma((2,)),
            dma((n,)), dma((n,)), dma((n,)), dma((n,)),
            dma((n,)), dma((n,)), dma((n,)), dma((n,)), dma((1,)), dma((1,)),
            dma((parts, nx)), dma((parts, nx)), dma((nx,)), dma((nx,)),
        ],
        compiler_params=pltpu.CompilerParams(
            collective_id=0, has_side_effects=True, vmem_limit_bytes=48 << 20
        ),
        name="directions",
    )(
        activations,
        cand_index.reshape(1, rows),
        labels.reshape(1, -1),
        counts.reshape(1, 1),
    )
    return out.T


def solution(mesh):
    n = 1
    while 2 * n * n < mesh.shape["dp"]:
        n *= 2
    return jax.shard_map(
        functools.partial(per_device, n, mesh.shape["feat"]),
        mesh=mesh,
        in_specs=(P("dp", "feat"), P("dp"), P("dp"), P("dp")),
        out_specs=P("dp", "feat"),
        check_vma=False,
    )
```

time: 620 us -> 65.6 us (0.11)
  blocking collectives: 566 us -> 0 us
  Pallas kernels: 0 us -> 60.5 us
  waiting for transfers between devices: 18.1 us -> 0 us
  between operations: 16.6 us -> 0.67 us
  matrix products: 8.01 us -> 0 us
    unnamed x2 -> x0, blocking collectives: 509 us -> none
    pallas_call x0 -> x1, Pallas kernels: none -> 60.5 us  [per_device(): pl.pallas_call(functools.partial(kernel, n, nx), out_shape=jax.ShapeDtype...]
    all_gather x1 -> x0, blocking collectives: 47.8 us -> none  [per_device(): dir_block = lax.all_gather(raw_dir, 'dp', axis=0, tiled=True)]
    reduce_scatter x1 -> x0, waiting for transfers between devices: 18.1 us -> none  [per_device(): lax.psum_scatter(partial_value, 'feat', scatter_dimension=1, tiled=True)]
    psum x1 -> x0, blocking collectives: 9.03 us -> none  [per_device(): total_sq = lax.psum(squares, 'feat')]
    dot_general x2 -> x0, matrix products: 8.01 us -> none  [the longest x1 4.57 us: project(): lax.dot_general(activations, dir_block, (((1,), (1,)), ((), ())), preferr...]
  transfers between devices with their start and end apart: 2 -> 0, of which waited for: 1 -> 0; matrix products, arithmetic and copies ran while one was open for 0% -> 0% of each run, Pallas kernels for 0% -> 0%
where the time goes in v1:
time: 65.6 us; the launch traced here: 65.4 us
  Pallas kernels  60.5 us (92%)
  local copies, waits for them, and re-layouts  4.18 us (6%)
  between operations  0.67 us (1%)
    pallas_call x1, Pallas kernels, per_device(): pl.pallas_call(functools.partial(kernel, n, nx), out_shape=jax.ShapeDtype...  60.5 us
    unnamed x7, local copies, waits for them, and re-layouts  4.18 us

profile of v1, /device:TPU:1, one launch (start us, length us, event | category | flops | bytes accessed | tf_op | source)
XLA Modules:
  0.0 65.4 jit_solution(3427345422853451665)
XLA Ops:
  0.7 0.0 copy-start
  0.7 2.2 %copy-done = bf16[1024,2048]{1,0:T(8,128)(2,1)S(1)} copy-done((bf16[1024,2048]{1,0:T(8,128)(2,1)S(1)}, bf16[1024,2048]{1,0:T(8,128)(2,1)}, u32[]{:S(2)}) %copy-start) | copy-done | bytes 4194328
  2.8 0.0 copy-start.1
  2.8 0.7 %copy-done.1 = s32[1024]{0:T(1024)S(1)} copy-done((s32[1024]{0:T(1024)S(1)}, s32[1024]{0:T(1024)}, u32[]{:S(2)}) %copy-start.1) | copy-done | bytes 4120
  3.5 0.0 copy-start.2
  3.5 0.7 copy-done.2
  4.2 60.5 %directions.1 = f32[32,1024]{1,0:T(8,128)S(1)} custom-call(bf16[1024,2048]{1,0:T(8,128)(2,1)S(1)} %copy-done, s32[1,1024]{1,0:T(1,128)S(1)} %bitcast.6, s32[1,64]{1,0:T(1,128)S(1)} %bitcast.7, s32[1,1]{1,0:T(1,128)} %bitcast.4.live_ref), custom_call_target="tpu_custom_call" | custom-call | tf_op jit(solution)/shard_map/directions/pallas_call | solution.py:304
  64.7 0.7 %copy.7 = f32[1024,32]{0,1:T(8,128)} copy(f32[1024,32]{0,1:T(8,128)S(1)} %bitcast.5) | data formatting | bytes 262144
Async XLA Ops:
  0.7 2.2 %copy-start = (bf16[1024,2048]{1,0:T(8,128)(2,1)S(1)}, bf16[1024,2048]{1,0:T(8,128)(2,1)}, u32[]{:S(2)}) copy-start(bf16[1024,2048]{1,0:T(8,128)(2,1)} %act_ref.1) | copy-start | bytes 12582916
  2.8 0.7 %copy-start.1 = (s32[1024]{0:T(1024)S(1)}, s32[1024]{0:T(1024)}, u32[]{:S(2)}) copy-start(s32[1024]{0:T(1024)} %param.5) | copy-start | bytes 12292
  3.5 0.7 %copy-start.2 = (s32[64]{0:T(128)S(1)}, s32[64]{0:T(128)}, u32[]{:S(2)}) copy-start(s32[64]{0:T(128)} %param.6) | copy-start | bytes 772
